TPU v7x, 32 devices: a whole 2x2x4 slice. The times are simulated.
32 devices in a mesh: tgt: 4 (over z), ptr: 8 (over y, x, core).
Axes of the slice: x: 2, y: 2, z: 4, core: 2. Of those that a mesh axis runs over, the one named last changes fastest.
Arguments:
- targets: float32 [32, 32, 1024], P('tgt'), may hold values from -12 to 12
- partners: float32 [32, 32, 1024], P(None, None, 'ptr'), may hold values from -6 to 6
- occupied: int32 [8], P('ptr'), may hold values 0 or 1
- retained: int32 [1], replicated, may hold values from 16 to 32
Outputs:
- compressed: float32 [32, 32, 1024], P('tgt', 'ptr')
All inputs are finite; a program needn't handle non-finite values. No bound on the sum of `occupied` on one device may be relied on, other than what follows from the above.
Results may differ from a plain program's by a relative error of at most 0.00008.
Values sent between devices are 32-bit elements; how exact they have to be, the bound alone decides.
A program may use at most 64 MiB of HBM per device.

v0:
```python
import functools
import math

import jax
import jax.numpy as jnp
import numpy as np
from jax import lax
from jax.experimental import pallas as pl
from jax.experimental.pallas import tpu as pltpu
from jax.sharding import PartitionSpec as P

HIGHEST = lax.Precision.HIGHEST
MESH = pl.DeviceIdType.MESH
FORWARD = 4
BACKWARD = 4


def real_dft(values):
    n = len(values)
    if n == 1:
        return [values[0]], [None]
    even_re, even_im = real_dft(values[0::2])
    odd_re, odd_im = real_dft(values[1::2])
    half = n // 2
    re, im = [None] * (half + 1), [None] * (half + 1)
    re[0], re[half] = even_re[0] + odd_re[0], even_re[0] - odd_re[0]
    for k in range(1, half // 2 + 1):
        if 2 * k == half:
            re[k], im[k] = even_re[k], -odd_re[k]
            continue
        c, s = math.cos(2 * math.pi * k / n), -math.sin(2 * math.pi * k / n)
        if 8 * k == n:
            a = c * (odd_re[k] + odd_im[k]) if odd_im[k] is not None else c * odd_re[k]
            b = c * (odd_im[k] - odd_re[k]) if odd_im[k] is not None else -c * odd_re[k]
        else:
            a = c * odd_re[k] - s * odd_im[k]
            b = s * odd_re[k] + c * odd_im[k]
        re[k], re[half - k] = even_re[k] + a, even_re[k] - a
        im[k], im[half - k] = even_im[k] + b, b - even_im[k]
    return re, im


def real_dft_transposed(re, im):
    half = len(re) - 1
    if half == 0:
        return [re[0]]
    n = 2 * half
    quarter = half // 2
    even_re, even_im = [None] * (quarter + 1), [None] * (quarter + 1)
    odd_re, odd_im = [None] * (quarter + 1), [None] * (quarter + 1)
    even_re[0], odd_re[0] = re[0] + re[half], re[0] - re[half]
    for k in range(1, quarter + 1):
        if 2 * k == half:
            even_re[k], odd_re[k] = re[k], -im[k]
            continue
        c, s = math.cos(2 * math.pi * k / n), -math.sin(2 * math.pi * k / n)
        even_re[k], even_im[k] = re[k] + re[half - k], im[k] - im[half - k]
        a, b = re[k] - re[half - k], im[k] + im[half - k]
        if 8 * k == n:
            odd_re[k], odd_im[k] = c * (a - b), c * (a + b)
        else:
            odd_re[k], odd_im[k] = c * a + s * b, c * b - s * a
    values = [None] * n
    values[0::2] = real_dft_transposed(even_re[: quarter + 1], even_im[: quarter + 1])
    values[1::2] = real_dft_transposed(odd_re[: quarter + 1], odd_im[: quarter + 1])
    return values


def flat_dft(values):
    re, im = real_dft(values)
    return re + im[1:-1]


def flat_dft_transposed(modes):
    half = len(modes) // 2
    return real_dft_transposed(modes[: half + 1], [None] + modes[half + 1 :] + [None])


def split_product(field, weights):
    width = field.shape[1]
    high = field.astype(jnp.bfloat16)
    low = (field - high.astype(jnp.float32)).astype(jnp.bfloat16)
    both = jnp.dot(
        jnp.concatenate([high, low], axis=1), weights, preferred_element_type=jnp.float32
    )
    return both[:, :width] + both[:, width:]


def kernel(
    tn, pn, t_hbm, psi_ref, weights_ref, table_ref, occupied_ref, retained_ref, out_ref,
    planes, spec, part, pair_buf, rs_buf, t_buf, a_buf, gram_ref, g_buf, inv_ref,
    load_sem, pair_send, pair_recv, rs_send, rs_recv, t_send, t_recv, a_send, a_recv, g_send, g_recv,
):
    t, p = lax.axis_index("tgt"), lax.axis_index("ptr")
    length, rows, cells = planes.shape
    lanes = psi_ref.shape[2]
    groups = lanes // length
    slab = length // pn
    all_cells = length * cells
    total_rows = tn * rows
    width = inv_ref.shape[1]
    me = t * pn + p
    devices = tn * pn
    chips = pn // 2
    chip, core = p // 2, lax.rem(p, 2)
    partner = p + 1 - 2 * core

    loads = [
        pltpu.make_async_copy(t_hbm.at[a], planes.at[:, a, :], load_sem.at[a]) for a in range(rows)
    ]
    for load in loads:
        load.start()

    barrier = pltpu.get_barrier_semaphore()

    @pl.loop(1, devices)
    def greet(d):
        other = lax.rem(me + d, devices)
        pl.semaphore_signal(
            barrier, inc=1, device_id=(other // pn, lax.rem(other, pn)), device_id_type=MESH
        )

    pl.semaphore_wait(barrier, devices - 1)
    for load in loads:
        load.wait()

    def pair_copy(q, r):
        return pltpu.make_async_remote_copy(
            src_ref=part.at[q * slab + r], dst_ref=pair_buf.at[q // 2, r],
            send_sem=pair_send.at[q // 2, r], recv_sem=pair_recv.at[q // 2, r],
            device_id=(t, partner), device_id_type=MESH,
        )

    def rs_copy(c, slot, r):
        q = 2 * c + core
        return pltpu.make_async_remote_copy(
            src_ref=part.at[q * slab + r], dst_ref=rs_buf.at[slot, r],
            send_sem=rs_send.at[c, r], recv_sem=rs_recv.at[slot, r],
            device_id=(t, q), device_id_type=MESH,
        )

    def t_copy(s, side, h):
        piece = pl.ds(h * (slab // 2), slab // 2)
        return pltpu.make_async_remote_copy(
            src_ref=t_buf.at[s, piece], dst_ref=t_buf.at[s, piece],
            send_sem=t_send.at[(side + 1) // 2, s, h], recv_sem=t_recv.at[s, h],
            device_id=(t + side, p), device_id_type=MESH,
        )

    def a_copy(s, side, r):
        return pltpu.make_async_remote_copy(
            src_ref=a_buf.at[s, r], dst_ref=a_buf.at[s, r],
            send_sem=a_send.at[(side + 1) // 2, s, r], recv_sem=a_recv.at[s, r],
            device_id=(t + side, p), device_id_type=MESH,
        )

    def relay(copy, hop, *at):
        for side in (-1, 1):
            s = t - side * (hop - 1)
            held = (s >= 0) & (s < tn)
            if hop > 1:

                @pl.when(held)
                def arrived():
                    copy(s, side, *at).wait_recv()

            if hop < tn:

                @pl.when(held & (t + side >= 0) & (t + side < tn))
                def onward():
                    copy(s, side, *at).start()

    def relayed(copy, *at):
        for side in (-1, 1):
            for hop in range(1, tn):
                s = t - side * (hop - 1)

                @pl.when((s >= 0) & (s < tn) & (t + side >= 0) & (t + side < tn))
                def sent():
                    copy(s, side, *at).wait_send()

    def g_copy(other, slot):
        return pltpu.make_async_remote_copy(
            src_ref=g_buf.at[me], dst_ref=g_buf.at[slot],
            send_sem=g_send.at[other], recv_sem=g_recv.at[slot],
            device_id=(other // pn, lax.rem(other, pn)), device_id_type=MESH,
        )

    t_buf[t] = planes[pl.ds(p * slab, slab)]
    relay(t_copy, 1, 0)
    relay(t_copy, 1, 1)

    group_of = lax.broadcasted_iota(jnp.int32, (rows, lanes), 1) // length
    at_group = [group_of == g for g in range(groups)]
    per_block = groups // occupied_ref.shape[0]
    occ = 0.25 + 0.75 * occupied_ref[0].astype(jnp.float32) * jnp.ones((rows, lanes), jnp.float32)
    for i in range(1, occupied_ref.shape[0]):
        level = 0.25 + 0.75 * occupied_ref[i].astype(jnp.float32)
        occ = jnp.where(group_of >= i * per_block, level, occ)

    def pick(options):
        chosen = options[0]
        for g in range(1, groups):
            chosen = jnp.where(at_group[g], options[g], chosen)
        return chosen

    def rolled(value, steps):
        steps = steps % groups
        return value if steps == 0 else pltpu.roll(value, steps * length, 1)

    plane_rows = length * rows

    @pl.loop(0, length // FORWARD)
    def forward(i):
        @pl.when(i == 3 * length // (4 * FORWARD))
        def second_hop():
            relay(t_copy, 2, 0)

        density = []
        for j in range(FORWARD):
            x = i * FORWARD + j
            for q in range(length // groups):
                v = planes[x, :, q * lanes : (q + 1) * lanes]
                turned = [rolled(v, s) for s in range(groups)]
                for g in range(groups):
                    y = q * groups + g
                    spread = pick([turned[(h - g) % groups] for h in range(groups)])
                    density.append(spread * psi_ref[x, y : y + 1, :])
        waves = split_product(jnp.concatenate(density, axis=0), weights_ref[...])
        for j in range(FORWARD):
            wave = waves[j * plane_rows : (j + 1) * plane_rows]
            modes = flat_dft([wave[y * rows : (y + 1) * rows] for y in range(length)])
            for m in range(length):
                spec[i * FORWARD + j, m] = modes[m]

    relay(t_copy, 2, 1)

    @pl.loop(0, length)
    def middle(m):
        @pl.when(m == length // 2)
        def third_hop():
            relay(t_copy, 3, 0)

        modes = flat_dft([spec[x, m] for x in range(length)])
        half = length // 2
        scaled = []
        for i in range(length):
            k = i if i <= half else i - half
            scaled.append(modes[i] * table_ref[m, k : k + 1, :])
        values = flat_dft_transposed(scaled)
        for x in range(length):
            spec[x, m] = values[x]

    gram_ref[...] = jnp.zeros_like(gram_ref)
    relay(t_copy, 3, 1)

    def relay_step(e):
        for hop in range(2, tn + 1):
            r = e - 2 * (hop - 1)
            if isinstance(e, int):
                if 0 <= r < slab:
                    relay(a_copy, hop, r)
            else:

                @pl.when(r >= 0)
                def earlier_round():
                    relay(a_copy, hop, r)

    def reduce_round(r):
        own = part[p * slab + r] + pair_buf[chip, r]
        for d in range(1, chips):
            c = lax.rem(chip + d, chips)
            rs_copy(c, c, r).wait_recv()
            own = own + rs_buf[c, r]
        a_buf[t, r] = own
        relay(a_copy, 1, r)
        relay_step(r)

    def add_gram(r):
        every = jnp.concatenate([t_buf[s, r] for s in range(tn)], axis=0)
        gram_ref[...] += lax.dot_general(
            a_buf[t, r], every, (((1,), (1,)), ((), ())),
            precision=HIGHEST, preferred_element_type=jnp.float32,
        )

    @pl.loop(0, slab)
    def rounds(r):
        @pl.loop(0, pn // BACKWARD)
        def backward(i):
            away = i < chips // BACKWARD
            first = lax.rem(i * BACKWARD, chips)
            side = jnp.where(away, 1 - core, core)
            owners = [
                2 * lax.rem(chip + 1 + first + j, chips) + side for j in range(BACKWARD)
            ]
            values = []
            for q in owners:
                values += flat_dft_transposed([spec[q * slab + r, m] for m in range(length)])
            potentials = split_product(jnp.concatenate(values, axis=0), weights_ref[...])
            for j, owner in enumerate(owners):
                x = owner * slab + r
                potential = potentials[j * plane_rows : (j + 1) * plane_rows]
                for q in range(length // groups):
                    terms = []
                    for g in range(groups):
                        y = q * groups + g
                        terms.append(potential[y * rows : (y + 1) * rows] * psi_ref[x, y : y + 1, :])
                    total = None
                    for s in range(groups):
                        chosen = pick([terms[(h - s) % groups] for h in range(groups)])
                        moved = rolled(chosen * occ, -s)
                        total = moved if total is None else total + moved
                    part[x, :, q * lanes : (q + 1) * lanes] = total

            @pl.when(away)
            def to_partner():
                for owner in owners:
                    pair_copy(owner, r).start()

            @pl.when(jnp.logical_not(away))
            def to_owners():
                for j, owner in enumerate(owners):
                    pair_copy(owner, r).wait_recv()

                    @pl.when(first + j < chips - 1)
                    def send():
                        x = owner * slab + r
                        part[x] = part[x] + pair_buf[owner // 2, r]
                        rs_copy(owner // 2, chip, r).start()

        @pl.when(r > 1)
        def earlier():
            reduce_round(r - 2)

    for hop in range(4, tn + 1):
        relay(t_copy, hop, 0)
        relay(t_copy, hop, 1)
    for r in range(slab - 2):
        add_gram(r)
    for r in range(slab - 2, slab):
        reduce_round(r)
        add_gram(r)

    gram = gram_ref[...] * (1.0 / all_cells)
    fold = 128 // total_rows
    short = rows // fold
    g_buf[me] = jnp.concatenate([gram[i * short : (i + 1) * short] for i in range(fold)], axis=1)

    @pl.loop(1, devices)
    def spread_gram(d):
        g_copy(lax.rem(me + d, devices), me).start()

    relay_step(slab)
    relay_step(slab + 1)

    @pl.loop(1, devices)
    def collect(d):
        other = lax.rem(me + d, devices)
        g_copy(other, other).wait_recv()

    relay_step(slab + 2)
    relay_step(slab + 3)
    blocks = []
    for s in range(tn):
        block = g_buf[s * pn]
        for q in range(1, pn):
            block = block + g_buf[s * pn + q]
        blocks += [block[:, i * total_rows : (i + 1) * total_rows] for i in range(fold)]
    square = jnp.concatenate(blocks, axis=0)
    square = jnp.concatenate(
        [square, jnp.zeros((total_rows, width - total_rows), jnp.float32)], axis=1
    )
    padded = jnp.concatenate([square, jnp.zeros((width - total_rows, width), jnp.float32)], axis=0)
    symmetric = 0.5 * (square + jnp.transpose(padded)[:total_rows])
    row_of = lax.broadcasted_iota(jnp.int32, (total_rows, width), 0)
    lane_of = lax.broadcasted_iota(jnp.int32, (total_rows, width), 1)
    work = jnp.where(lane_of == row_of + total_rows, 1.0, symmetric)
    for k in range(total_rows - 1):
        row = work[k : k + 1, :]
        scaled = row / work[k : k + 1, k : k + 1]
        column = jnp.where(row_of > k, work[:, k : k + 1], 0.0)
        work = work - column * scaled
    pivots = jnp.sum(jnp.where(lane_of == row_of, work, 0.0), axis=1, keepdims=True)
    keeping = (row_of < retained_ref[0]).astype(jnp.float32)
    inv_ref[...] = work * (1.0 / jnp.sqrt(pivots)) * keeping
    mine = inv_ref[pl.ds(pl.multiple_of(t * rows, rows), rows), :][:, total_rows : 2 * total_rows]
    for e in range(slab + 4, slab + 2 * (tn - 1)):
        relay_step(e)
    for x in range(slab):
        every = jnp.concatenate([a_buf[s, x] for s in range(tn)], axis=0)
        out_ref[:, x, :] = jnp.dot(
            mine, every, precision=HIGHEST, preferred_element_type=jnp.float32
        )

    relayed(t_copy, 0)
    relayed(t_copy, 1)
    for r in range(slab):
        for c in range(chips):
            pair_copy(2 * c + 1 - core, r).wait_send()
        for d in range(1, chips):
            rs_copy(lax.rem(chip + d, chips), chip, r).wait_send()
        relayed(a_copy, r)

    @pl.loop(1, devices)
    def drain(d):
        g_copy(lax.rem(me + d, devices), me).wait_send()


def constants(length, groups):
    i = np.arange(length)
    phase = 2.0 * np.pi / length * (i[:, None] * i[None, :] % length)
    cas = np.kron(np.eye(groups), np.cos(phase) + np.sin(phase)).astype(np.float32)
    high = cas.astype(jnp.bfloat16)
    low = (cas - high.astype(np.float32)).astype(jnp.bfloat16)
    weights = np.concatenate([np.concatenate([high, low], 1)] * 2, 0)
    signed = np.where(i < length // 2, i, i - length)
    half = length // 2
    k = np.arange(half + 1)
    wave = (2.0 * np.pi / length) ** 2
    total = wave * ((k**2)[:, None, None] + (k**2)[None, :, None] + (signed**2)[None, None, :])
    coulomb = np.where(total > 0, 4 * np.pi / np.where(total > 0, total, 1.0), 0.0)
    fold = np.where((k == 0) | (k == half), 1.0, 2.0)
    coulomb = coulomb * fold[:, None, None] * fold[None, :, None] / length**3
    order = np.concatenate([np.arange(half + 1), np.arange(1, half)])
    table = np.tile(coulomb[order], (1, 1, groups)).astype(np.float32)
    return weights, table


def shards(tn, pn, targets, partners, occupied, retained):
    rows, length, cells = targets.shape
    lanes = partners.shape[2]
    groups = lanes // length
    slab = length // pn
    weights, table = constants(length, groups)
    total_rows = tn * rows
    width = -(-2 * total_rows // 128) * 128
    vmem = pl.BlockSpec(memory_space=pltpu.VMEM)
    smem = pl.BlockSpec(memory_space=pltpu.SMEM)
    dma = pltpu.SemaphoreType.DMA
    planes = pltpu.VMEM((length, rows, cells), jnp.float32)
    block = pltpu.VMEM((tn, slab, rows, cells), jnp.float32)
    return pl.pallas_call(
        functools.partial(kernel, tn, pn),
        out_shape=jax.ShapeDtypeStruct((rows, slab, cells), jnp.float32),
        in_specs=[pl.BlockSpec(memory_space=pl.ANY), vmem, vmem, vmem, smem, smem],
        out_specs=vmem,
        scratch_shapes=[
            planes,
            pltpu.VMEM((length, length, rows, lanes), jnp.float32),
            planes,
            pltpu.VMEM((pn // 2, slab, rows, cells), jnp.float32),
            pltpu.VMEM((pn // 2, slab, rows, cells), jnp.float32),
            block,
            block,
            pltpu.VMEM((rows, total_rows), jnp.float32),
            pltpu.VMEM((tn * pn, rows * total_rows // 128, 128), jnp.float32),
            pltpu.VMEM((total_rows, width), jnp.float32),
            dma((rows,)), dma((pn // 2, slab)), dma((pn // 2, slab)), dma((pn // 2, slab)),
            dma((pn // 2, slab)), dma((2, tn, 2)), dma((tn, 2)), dma((2, tn, slab)), dma((tn, slab)), dma((tn * pn,)), dma((tn * pn,)),
        ],
        compiler_params=pltpu.CompilerParams(collective_id=0, has_side_effects=True),
        name="exchange",
    )(targets, partners, jnp.asarray(weights), jnp.asarray(table), occupied, retained)


def solution(mesh):
    return jax.shard_map(
        functools.partial(shards, mesh.shape["tgt"], mesh.shape["ptr"]),
        mesh=mesh,
        in_specs=(P("tgt", None, None), P(None, None, "ptr"), P("ptr"), P()),
        out_specs=P("tgt", "ptr", None),
        check_vma=False,
    )
```

profile of v0, /device:TPU:0, one launch (start us, length us, event | category | flops | bytes accessed | tf_op | source)
XLA Modules:
  0.0 43.6 jit_solution(13279975571868788306)
XLA Ops:
  1.3 40.7 %exchange.1 = f32[8,4,1024]{2,1,0:T(4,128)} custom-call(f32[8,32,1024]{2,1,0:T(8,128)} %t_hbm.1, f32[32,32,128]{2,1,0:T(8,128)} %psi_ref.1, bf16[256,256]{1,0:T(8,128)(2,1)} %constant.4.clone.weights_ref, f32[32,17,128]{2,1,0:T(8,128)} %constant.5.clone.table_ref, s32[1]{0:T(128)S(6)} %copy.8.occupied_ref, s32[1]{0:T(128)S(6)} %copy.9.retained_ref), custom_call_target="tpu_custom_call" | custom-call | tf_op jit(solution)/shard_map/exchange/pallas_call | solution.py:442
  42.0 1.6 %copy.10 = f32[8,4,1024]{2,1,0:T(4,128)} copy(f32[8,4,1024]{2,1,0:T(4,128)} %exchange.1) | data formatting | bytes 262144
where the time goes:
time: 43.7 us; the launch traced here: 43.6 us
  Pallas kernels  40.7 us (93%)
  local copies, waits for them, and re-layouts  1.57 us (4%)
  between operations  1.3 us (3%)
    pallas_call x1, Pallas kernels, shards(): pl.pallas_call(functools.partial(kernel, tn, pn), out_shape=jax.ShapeDtyp...  40.7 us
    unnamed x1, local copies, waits for them, and re-layouts  1.57 us

commit v1 on v0

v1 whole, which is shorter than its diff:
```python
import functools
import math

import jax
import jax.numpy as jnp
import numpy as np
from jax import lax
from jax.experimental import pallas as pl
from jax.experimental.pallas import tpu as pltpu
from jax.sharding import PartitionSpec as P

HIGHEST = lax.Precision.HIGHEST
MESH = pl.DeviceIdType.MESH
FORWARD = 4
BACKWARD = 4
PIVOTS = 4


def real_dft(values):
    n = len(values)
    if n == 1:
        return [values[0]], [None]
    even_re, even_im = real_dft(values[0::2])
    odd_re, odd_im = real_dft(values[1::2])
    half = n // 2
    re, im = [None] * (half + 1), [None] * (half + 1)
    re[0], re[half] = even_re[0] + odd_re[0], even_re[0] - odd_re[0]
    for k in range(1, half // 2 + 1):
        if 2 * k == half:
            re[k], im[k] = even_re[k], -odd_re[k]
            continue
        c, s = math.cos(2 * math.pi * k / n), -math.sin(2 * math.pi * k / n)
        if 8 * k == n:
            a = c * (odd_re[k] + odd_im[k]) if odd_im[k] is not None else c * odd_re[k]
            b = c * (odd_im[k] - odd_re[k]) if odd_im[k] is not None else -c * odd_re[k]
        else:
            a = c * odd_re[k] - s * odd_im[k]
            b = s * odd_re[k] + c * odd_im[k]
        re[k], re[half - k] = even_re[k] + a, even_re[k] - a
        im[k], im[half - k] = even_im[k] + b, b - even_im[k]
    return re, im


def real_dft_transposed(re, im):
    half = len(re) - 1
    if half == 0:
        return [re[0]]
    n = 2 * half
    quarter = half // 2
    even_re, even_im = [None] * (quarter + 1), [None] * (quarter + 1)
    odd_re, odd_im = [None] * (quarter + 1), [None] * (quarter + 1)
    even_re[0], odd_re[0] = re[0] + re[half], re[0] - re[half]
    for k in range(1, quarter + 1):
        if 2 * k == half:
            even_re[k], odd_re[k] = re[k], -im[k]
            continue
        c, s = math.cos(2 * math.pi * k / n), -math.sin(2 * math.pi * k / n)
        even_re[k], even_im[k] = re[k] + re[half - k], im[k] - im[half - k]
        a, b = re[k] - re[half - k], im[k] + im[half - k]
        if 8 * k == n:
            odd_re[k], odd_im[k] = c * (a - b), c * (a + b)
        else:
            odd_re[k], odd_im[k] = c * a + s * b, c * b - s * a
    values = [None] * n
    values[0::2] = real_dft_transposed(even_re[: quarter + 1], even_im[: quarter + 1])
    values[1::2] = real_dft_transposed(odd_re[: quarter + 1], odd_im[: quarter + 1])
    return values


def flat_dft(values):
    re, im = real_dft(values)
    return re + im[1:-1]


def flat_dft_transposed(modes):
    half = len(modes) // 2
    return real_dft_transposed(modes[: half + 1], [None] + modes[half + 1 :] + [None])


def split_product(field, weights):
    width = field.shape[1]
    high = field.astype(jnp.bfloat16)
    low = (field - high.astype(jnp.float32)).astype(jnp.bfloat16)
    both = jnp.dot(
        jnp.concatenate([high, low], axis=1), weights, preferred_element_type=jnp.float32
    )
    return both[:, :width] + both[:, width:]


def kernel(
    tn, pn, t_hbm, psi_hbm, weights_hbm, table_hbm, occupied_ref, retained_ref, out_ref,
    planes, psi_ref, weights_ref, table_ref, spec, part, pair_buf, rs_buf, t_buf, a_buf,
    gram_ref, g_buf, inv_ref,
):
    slab = planes.shape[0] // pn
    rows = planes.shape[1]
    dma = pltpu.SemaphoreType.DMA
    pl.run_scoped(
        functools.partial(
            exchange, tn, pn, t_hbm, psi_hbm, weights_hbm, table_hbm, occupied_ref, retained_ref,
            out_ref, planes, psi_ref, weights_ref, table_ref, spec, part, pair_buf, rs_buf, t_buf,
            a_buf, gram_ref, g_buf, inv_ref,
        ),
        dma((2, rows)), dma((4,)), dma((pn // 2, slab)), dma((pn // 2, slab)),
        dma((pn // 2, slab)), dma((pn // 2, slab)), dma((tn,)), dma((tn,)),
        dma((tn, tn, slab)), dma((tn, slab)), dma((tn,)), dma((tn,)),
    )


def exchange(
    tn, pn, t_hbm, psi_hbm, weights_hbm, table_hbm, occupied_ref, retained_ref, out_ref,
    planes, psi_ref, weights_ref, table_ref, spec, part, pair_buf, rs_buf, t_buf, a_buf,
    gram_ref, g_buf, inv_ref,
    plane_sem, load_sem, pair_send, pair_recv, rs_send, rs_recv, t_send, t_recv,
    a_send, a_recv, g_send, g_recv,
):
    t, p = lax.axis_index("tgt"), lax.axis_index("ptr")
    length, rows, cells = planes.shape
    lanes = psi_ref.shape[2]
    groups = lanes // length
    slab = length // pn
    all_cells = length * cells
    total_rows = tn * rows
    width = inv_ref.shape[1]
    me = t * pn + p
    chips = pn // 2
    chip, core = p // 2, lax.rem(p, 2)
    partner = p + 1 - 2 * core
    early = length // 4

    def plane_load(c, a):
        xs = pl.ds(0, early) if c == 0 else pl.ds(early, length - early)
        return pltpu.make_async_copy(t_hbm.at[a, xs, :], planes.at[xs, a, :], plane_sem.at[c, a])

    def psi_load(c):
        xs = pl.ds(0, early) if c == 0 else pl.ds(early, length - early)
        return pltpu.make_async_copy(psi_hbm.at[xs], psi_ref.at[xs], load_sem.at[c])

    weights_load = pltpu.make_async_copy(weights_hbm, weights_ref, load_sem.at[2])
    table_load = pltpu.make_async_copy(table_hbm, table_ref, load_sem.at[3])

    weights_load.start()
    for c in range(2):
        psi_load(c).start()
        for a in range(rows):
            plane_load(c, a).start()
    table_load.start()

    barrier = pltpu.get_barrier_semaphore()
    for tt in range(tn):
        for pp in range(pn):

            @pl.when((t != tt) | (p != pp))
            def greet():
                pl.semaphore_signal(barrier, inc=1, device_id=(tt, pp), device_id_type=MESH)

    def pair_copy(q, r):
        return pltpu.make_async_remote_copy(
            src_ref=part.at[q * slab + r], dst_ref=pair_buf.at[q // 2, r],
            send_sem=pair_send.at[q // 2, r], recv_sem=pair_recv.at[q // 2, r],
            device_id=(t, partner), device_id_type=MESH,
        )

    def rs_copy(c, slot, r):
        q = 2 * c + core
        return pltpu.make_async_remote_copy(
            src_ref=part.at[q * slab + r], dst_ref=rs_buf.at[slot, r],
            send_sem=rs_send.at[c, r], recv_sem=rs_recv.at[slot, r],
            device_id=(t, q), device_id_type=MESH,
        )

    def t_copy(d, source, target):
        return pltpu.make_async_remote_copy(
            src_ref=planes.at[pl.ds(p * slab, slab)], dst_ref=t_buf.at[source],
            send_sem=t_send.at[d], recv_sem=t_recv.at[d],
            device_id=(target, p), device_id_type=MESH,
        )

    def t_sends(act):
        for d in range(1, tn):
            target = t + d if d % 2 else t - d

            @pl.when((target >= 0) & (target < tn))
            def send():
                act(t_copy(d, t, target))

    def t_arrivals():
        for d in range(1, tn):
            source = t - d if d % 2 else t + d

            @pl.when((source >= 0) & (source < tn))
            def arrived():
                t_copy(d, source, t).wait_recv()

    def a_copy(s, target, r):
        return pltpu.make_async_remote_copy(
            src_ref=a_buf.at[s, r], dst_ref=a_buf.at[s, r],
            send_sem=a_send.at[s, target, r], recv_sem=a_recv.at[s, r],
            device_id=(target, p), device_id_type=MESH,
        )

    def a_route(r, act):
        for s in range(tn - 1):
            for target in range(s + 1, tn):
                if s % 2 == 0 or target == s + 1:

                    @pl.when(t == s)
                    def direct():
                        act(a_copy(s, target, r))

    def a_onward(r, act, wait):
        for s in range(1, tn - 2, 2):

            @pl.when(t == s + 1)
            def onward():
                if wait:
                    a_copy(s, s + 1, r).wait_recv()
                for target in range(s + 2, tn):
                    act(a_copy(s, target, r))

    def a_arrivals():
        for s in range(tn - 1):
            if s % 2 == 1 and s + 2 < tn:
                here = t > s + 1
            else:
                here = t > s

            @pl.when(here)
            def arrived():
                for r in range(slab):
                    a_copy(s, s + 1, r).wait_recv()

    def start(copy):
        copy.start()

    def sent(copy):
        copy.wait_send()

    def g_copy(target, q):
        return pltpu.make_async_remote_copy(
            src_ref=g_buf.at[me], dst_ref=g_buf.at[me],
            send_sem=g_send.at[target], recv_sem=g_recv.at[t],
            device_id=(target, q), device_id_type=MESH,
        )

    def g_all(s, count):
        every = g_buf.at[pl.ds(s * pn, count)]
        return pltpu.make_async_remote_copy(
            src_ref=every, dst_ref=every, send_sem=g_send.at[s], recv_sem=g_recv.at[s],
            device_id=(t, partner), device_id_type=MESH,
        )

    group_of = lax.broadcasted_iota(jnp.int32, (rows, lanes), 1) // length
    at_group = [group_of == g for g in range(groups)]
    per_block = groups // occupied_ref.shape[0]
    occ = 0.25 + 0.75 * occupied_ref[0].astype(jnp.float32) * jnp.ones((rows, lanes), jnp.float32)
    for i in range(1, occupied_ref.shape[0]):
        level = 0.25 + 0.75 * occupied_ref[i].astype(jnp.float32)
        occ = jnp.where(group_of >= i * per_block, level, occ)

    def pick(options):
        chosen = options[0]
        for g in range(1, groups):
            chosen = jnp.where(at_group[g], options[g], chosen)
        return chosen

    def rolled(value, steps):
        steps = steps % groups
        return value if steps == 0 else pltpu.roll(value, steps * length, 1)

    plane_rows = length * rows

    weights_load.wait()
    psi_load(0).wait()
    for a in range(rows):
        plane_load(0, a).wait()

    @pl.loop(0, length // FORWARD)
    def forward(i):
        @pl.when(i == early // FORWARD)
        def rest():
            psi_load(1).wait()
            for a in range(rows):
                plane_load(1, a).wait()

        density = []
        for j in range(FORWARD):
            x = i * FORWARD + j
            for q in range(length // groups):
                v = planes[x, :, q * lanes : (q + 1) * lanes]
                turned = [rolled(v, s) for s in range(groups)]
                for g in range(groups):
                    y = q * groups + g
                    spread = pick([turned[(h - g) % groups] for h in range(groups)])
                    density.append(spread * psi_ref[x, y : y + 1, :])
        waves = split_product(jnp.concatenate(density, axis=0), weights_ref[...])
        for j in range(FORWARD):
            wave = waves[j * plane_rows : (j + 1) * plane_rows]
            modes = flat_dft([wave[y * rows : (y + 1) * rows] for y in range(length)])
            for m in range(length):
                spec[i * FORWARD + j, m] = modes[m]

    t_buf[t] = planes[pl.ds(p * slab, slab)]
    for s in range(1, tn):

        @pl.when(s > t)
        def clear():
            a_buf[s] = jnp.zeros(a_buf.shape[1:], jnp.float32)

    gram_ref[...] = jnp.zeros_like(gram_ref)
    table_load.wait()
    pl.semaphore_wait(barrier, tn * pn - 1)
    t_sends(start)

    @pl.loop(0, length)
    def middle(m):
        modes = flat_dft([spec[x, m] for x in range(length)])
        half = length // 2
        scaled = []
        for i in range(length):
            k = i if i <= half else i - half
            scaled.append(modes[i] * table_ref[m, k : k + 1, :])
        values = flat_dft_transposed(scaled)
        for x in range(length):
            spec[x, m] = values[x]

    per = chips // BACKWARD

    @pl.loop(0, 2 * slab * per)
    def backward(n):
        i = n // per
        first = lax.rem(n, per) * BACKWARD
        odd = lax.rem(i, 2)
        last = i == 2 * slab - 1
        away = (i == 0) | ((odd == 1) & jnp.logical_not(last))
        r = jnp.where(away, (i + 1) // 2, jnp.where(last, slab - 1, i // 2 - 1))
        side = jnp.where(away, 1 - core, core)
        owners = [2 * lax.rem(chip + 1 + first + j, chips) + side for j in range(BACKWARD)]
        values = []
        for q in owners:
            values += flat_dft_transposed([spec[q * slab + r, m] for m in range(length)])
        potentials = split_product(jnp.concatenate(values, axis=0), weights_ref[...])
        for j, owner in enumerate(owners):
            x = owner * slab + r
            potential = potentials[j * plane_rows : (j + 1) * plane_rows]
            for q in range(length // groups):
                terms = []
                for g in range(groups):
                    y = q * groups + g
                    terms.append(potential[y * rows : (y + 1) * rows] * psi_ref[x, y : y + 1, :])
                total = None
                for s in range(groups):
                    chosen = pick([terms[(h - s) % groups] for h in range(groups)])
                    moved = rolled(chosen * occ, -s)
                    total = moved if total is None else total + moved
                part[x, :, q * lanes : (q + 1) * lanes] = total

        @pl.when(away)
        def to_partner():
            for owner in owners:
                pair_copy(owner, r).start()

        @pl.when(jnp.logical_not(away))
        def to_owners():
            for j, owner in enumerate(owners):
                pair_copy(owner, r).wait_recv()

                @pl.when(first + j < chips - 1)
                def send():
                    x = owner * slab + r
                    part[x] = part[x] + pair_buf[owner // 2, r]
                    rs_copy(owner // 2, chip, r).start()

    t_arrivals()

    @pl.loop(0, slab)
    def reduce(r):
        own = part[p * slab + r] + pair_buf[chip, r]
        for d in range(1, chips):
            c = lax.rem(chip + d, chips)
            rs_copy(c, c, r).wait_recv()
            own = own + rs_buf[c, r]
        a_buf[t, r] = own
        a_route(r, start)
        every = jnp.concatenate([t_buf[s, r] for s in range(tn)], axis=0)
        gram_ref[...] += lax.dot_general(
            own, every, (((1,), (1,)), ((), ())),
            precision=HIGHEST, preferred_element_type=jnp.float32,
        )

        @pl.when(r > 0)
        def earlier():
            a_onward(r - 1, start, True)

    gram = gram_ref[...] * (1.0 / all_cells)
    fold = 128 // total_rows
    short = rows // fold
    g_buf[me] = jnp.concatenate([gram[i * short : (i + 1) * short] for i in range(fold)], axis=1)

    for target in reversed(range(tn)):
        for q in range(pn):

            @pl.when((t < target) | ((t == target) & (p != q)))
            def spread():
                g_copy(target, q).start()

    a_onward(slab - 1, start, True)
    t_sends(sent)

    @pl.loop(0, slab)
    def drain(r):
        for c in range(chips):
            pair_copy(2 * c + 1 - core, r).wait_send()
        for d in range(1, chips):
            rs_copy(lax.rem(chip + d, chips), chip, r).wait_send()

    for s in range(tn):

        @pl.when(t > s)
        def others():
            g_all(s, pn).wait_recv()

        @pl.when(t == s)
        def mates():
            g_all(s, pn - 1).wait_recv()

    blocks = []
    for s in range(tn):
        block = g_buf[s * pn]
        for q in range(1, pn):
            block = block + g_buf[s * pn + q]
        blocks += [block[:, i * total_rows : (i + 1) * total_rows] for i in range(fold)]
    square = jnp.concatenate(blocks, axis=0)
    square = jnp.concatenate(
        [square, jnp.zeros((total_rows, width - total_rows), jnp.float32)], axis=1
    )
    row_of = lax.broadcasted_iota(jnp.int32, (total_rows, width), 0)
    lane_of = lax.broadcasted_iota(jnp.int32, (total_rows, width), 1)
    row_block, lane_block = row_of // rows, lane_of // rows
    apart = lane_block - row_block
    odd = lax.rem(jnp.abs(apart), 2) == 1
    held = (apart == 0) | ((apart < 0) & odd) | ((apart > 0) & jnp.logical_not(odd))
    held = held & (row_block <= t) & (lane_block <= t)
    square = jnp.where(held, square, 0.0)
    padded = jnp.concatenate([square, jnp.zeros((width - total_rows, width), jnp.float32)], axis=0)
    both = square + jnp.transpose(padded)[:total_rows]
    symmetric = jnp.where(apart == 0, 0.5 * both, both)
    unit = (lane_of == row_of + total_rows) | ((lane_of == row_of) & (row_block > t))
    work = jnp.where(unit, 1.0, symmetric)
    scale = jnp.zeros((total_rows, width), jnp.float32)
    for k in range(0, total_rows, PIVOTS):
        columns = [
            jnp.broadcast_to(work[:, k + i : k + i + 1], (total_rows, width)) for i in range(PIVOTS)
        ]
        lines = [work[k + i : k + i + 1, :] for i in range(PIVOTS)]
        corner = [[columns[j][k + i : k + i + 1, :] for j in range(PIVOTS)] for i in range(PIVOTS)]
        for i in range(PIVOTS):
            pivot = corner[i][i]
            scale = jnp.where(row_of == k + i, 1.0 / jnp.sqrt(pivot), scale)
            inverse = 1.0 / pivot
            scaled = lines[i] * inverse
            for m in range(i + 1, PIVOTS):
                factor = corner[i][m] * inverse
                columns[m] = columns[m] - columns[i] * factor
                lines[m] = lines[m] - corner[m][i] * scaled
                for h in range(i + 1, PIVOTS):
                    corner[h][m] = corner[h][m] - corner[h][i] * factor
            work = work - jnp.where(row_of > k + i, columns[i], 0.0) * scaled
    keeping = (row_of < retained_ref[0]).astype(jnp.float32)
    inv_ref[...] = work * scale * keeping
    mine = inv_ref[pl.ds(pl.multiple_of(t * rows, rows), rows), :][:, total_rows : 2 * total_rows]
    a_arrivals()
    for x in range(slab):
        every = jnp.concatenate([a_buf[s, x] for s in range(tn)], axis=0)
        out_ref[:, x, :] = jnp.dot(
            mine, every, precision=HIGHEST, preferred_element_type=jnp.float32
        )

    for target in range(tn):

        @pl.when(t < target)
        def upward():
            g_all(target, pn).wait_send()

        @pl.when(t == target)
        def within():
            g_all(target, pn - 1).wait_send()

    for r in range(slab):
        a_route(r, sent)
        a_onward(r, sent, False)


def constants(length, groups):
    i = np.arange(length)
    phase = 2.0 * np.pi / length * (i[:, None] * i[None, :] % length)
    cas = np.kron(np.eye(groups), np.cos(phase) + np.sin(phase)).astype(np.float32)
    high = cas.astype(jnp.bfloat16)
    low = (cas - high.astype(np.float32)).astype(jnp.bfloat16)
    weights = np.concatenate([np.concatenate([high, low], 1)] * 2, 0)
    signed = np.where(i < length // 2, i, i - length)
    half = length // 2
    k = np.arange(half + 1)
    wave = (2.0 * np.pi / length) ** 2
    total = wave * ((k**2)[:, None, None] + (k**2)[None, :, None] + (signed**2)[None, None, :])
    coulomb = np.where(total > 0, 4 * np.pi / np.where(total > 0, total, 1.0), 0.0)
    fold = np.where((k == 0) | (k == half), 1.0, 2.0)
    coulomb = coulomb * fold[:, None, None] * fold[None, :, None] / length**3
    order = np.concatenate([np.arange(half + 1), np.arange(1, half)])
    table = np.tile(coulomb[order], (1, 1, groups)).astype(np.float32)
    return weights, table


def shards(tn, pn, targets, partners, occupied, retained):
    rows, length, cells = targets.shape
    lanes = partners.shape[2]
    groups = lanes // length
    slab = length // pn
    weights, table = constants(length, groups)
    total_rows = tn * rows
    width = -(-2 * total_rows // 128) * 128
    vmem = pl.BlockSpec(memory_space=pltpu.VMEM)
    smem = pl.BlockSpec(memory_space=pltpu.SMEM)
    hbm = pl.BlockSpec(memory_space=pl.ANY)
    planes = pltpu.VMEM((length, rows, cells), jnp.float32)
    block = pltpu.VMEM((tn, slab, rows, cells), jnp.float32)
    received = pltpu.VMEM((pn // 2, slab, rows, cells), jnp.float32)
    return pl.pallas_call(
        functools.partial(kernel, tn, pn),
        out_shape=pltpu.VMEM((rows, slab, cells), jnp.float32),
        in_specs=[hbm, hbm, hbm, hbm, smem, smem],
        out_specs=vmem,
        scratch_shapes=[
            planes,
            pltpu.VMEM(partners.shape, jnp.float32),
            pltpu.VMEM(weights.shape, weights.dtype),
            pltpu.VMEM(table.shape, jnp.float32),
            pltpu.VMEM((length, length, rows, lanes), jnp.float32),
            planes,
            received,
            received,
            block,
            block,
            pltpu.VMEM((rows, total_rows), jnp.float32),
            pltpu.VMEM((tn * pn, rows * total_rows // 128, 128), jnp.float32),
            pltpu.VMEM((total_rows, width), jnp.float32),
        ],
        compiler_params=pltpu.CompilerParams(collective_id=0, has_side_effects=True),
        name="exchange",
    )(targets, partners, jnp.asarray(weights), jnp.asarray(table), occupied, retained)


def solution(mesh):
    return jax.shard_map(
        functools.partial(shards, mesh.shape["tgt"], mesh.shape["ptr"]),
        mesh=mesh,
        in_specs=(P("tgt", None, None), P(None, None, "ptr"), P("ptr"), P()),
        out_specs=P("tgt", "ptr", None),
        check_vma=False,
    )
```

time: 43.7 us -> 28.7 us (0.66)
  the two profiles are of different devices: /device:TPU:0 before, /device:TPU:25 now
where the time goes in v1:
time: 28.7 us; the launch traced here: 28.1 us
  Pallas kernels  26.1 us (91%)
  between operations  1.3 us (5%)
  local copies, waits for them, and re-layouts  0.66 us (2%)
    pallas_call x1, Pallas kernels, shards(): pl.pallas_call(functools.partial(kernel, tn, pn), out_shape=pltpu.VMEM((r...  26.1 us
    unnamed x1, local copies, waits for them, and re-layouts  0.66 us

profile of v1, /device:TPU:25, one launch (start us, length us, event | category | flops | bytes accessed | tf_op | source)
XLA Modules:
  0.0 28.1 jit_solution(1705902657115371493)
XLA Ops:
  1.3 26.1 %exchange.1 = f32[8,4,1024]{2,1,0:T(4,128)S(1)} custom-call(f32[8,32,1024]{2,1,0:T(8,128)} %t_hbm.1, f32[32,32,128]{2,1,0:T(8,128)} %psi_hbm.1, bf16[256,256]{1,0:T(8,128)(2,1)} %constant.4.clone.weights_hbm, f32[32,17,128]{2,1,0:T(8,128)} %constant.5.clone.table_hbm, s32[1]{0:T(128)S(6)} %copy.9.occupied_ref, s32[1]{0:T(128)S(6)} %copy.10.retained_ref), custom_call_target="tpu_custom_call" | custom-call | tf_op jit(solution)/shard_map/exchange/pallas_call | solution.py:528
  27.4 0.7 %copy.8 = f32[8,4,1024]{2,1,0:T(4,128)} copy(f32[8,4,1024]{2,1,0:T(4,128)S(1)} %exchange.1) | data formatting | bytes 262144

commit v2 on v1

--- a/solution.py
+++ b/solution.py
@@ -11,33 +11,47 @@
 
 HIGHEST = lax.Precision.HIGHEST
 MESH = pl.DeviceIdType.MESH
-FORWARD = 4
+FORWARD = 8
 BACKWARD = 4
 PIVOTS = 4
+HELD = 2
+
+
+def turned_by(n, k, re, im):
+    c, s = math.cos(2 * math.pi * k / n), math.sin(2 * math.pi * k / n)
+    return c * re + s * im, c * im - s * re
 
 
 def real_dft(values):
     n = len(values)
     if n == 1:
         return [values[0]], [None]
+    if n == 2:
+        return [values[0] + values[1], values[0] - values[1]], [None, None]
+    half, quarter, eighth = n // 2, n // 4, n // 8
     even_re, even_im = real_dft(values[0::2])
-    odd_re, odd_im = real_dft(values[1::2])
-    half = n // 2
+    one_re, one_im = real_dft(values[1::4])
+    three_re, three_im = real_dft(values[3::4])
     re, im = [None] * (half + 1), [None] * (half + 1)
-    re[0], re[half] = even_re[0] + odd_re[0], even_re[0] - odd_re[0]
-    for k in range(1, half // 2 + 1):
-        if 2 * k == half:
-            re[k], im[k] = even_re[k], -odd_re[k]
+    total = one_re[0] + three_re[0]
+    re[0], re[half] = even_re[0] + total, even_re[0] - total
+    re[quarter], im[quarter] = even_re[quarter], three_re[0] - one_re[0]
+    for k in range(1, eighth + 1):
+        if 2 * k == quarter:
+            c = math.sqrt(0.5)
+            a, b = c * (one_re[k] - three_re[k]), c * (one_re[k] + three_re[k])
+            re[k], re[half - k] = even_re[k] + a, even_re[k] - a
+            im[k], im[half - k] = even_im[k] - b, -b - even_im[k]
             continue
-        c, s = math.cos(2 * math.pi * k / n), -math.sin(2 * math.pi * k / n)
-        if 8 * k == n:
-            a = c * (odd_re[k] + odd_im[k]) if odd_im[k] is not None else c * odd_re[k]
-            b = c * (odd_im[k] - odd_re[k]) if odd_im[k] is not None else -c * odd_re[k]
-        else:
-            a = c * odd_re[k] - s * odd_im[k]
-            b = s * odd_re[k] + c * odd_im[k]
-        re[k], re[half - k] = even_re[k] + a, even_re[k] - a
-        im[k], im[half - k] = even_im[k] + b, b - even_im[k]
+        one = turned_by(n, k, one_re[k], one_im[k])
+        three = turned_by(n, 3 * k, three_re[k], three_im[k])
+        sum_re, sum_im = one[0] + three[0], one[1] + three[1]
+        gap_re, gap_im = one[0] - three[0], one[1] - three[1]
+        re[k], re[half - k] = even_re[k] + sum_re, even_re[k] - sum_re
+        im[k], im[half - k] = even_im[k] + sum_im, sum_im - even_im[k]
+        mirror = quarter - k
+        re[quarter + k], re[mirror] = even_re[mirror] + gap_im, even_re[mirror] - gap_im
+        im[quarter + k], im[mirror] = -gap_re - even_im[mirror], even_im[mirror] - gap_re
     return re, im
 
 
@@ -45,25 +59,35 @@
     half = len(re) - 1
     if half == 0:
         return [re[0]]
+    if half == 1:
+        return [re[0] + re[1], re[0] - re[1]]
     n = 2 * half
-    quarter = half // 2
+    quarter, eighth = half // 2, half // 4
     even_re, even_im = [None] * (quarter + 1), [None] * (quarter + 1)
-    odd_re, odd_im = [None] * (quarter + 1), [None] * (quarter + 1)
-    even_re[0], odd_re[0] = re[0] + re[half], re[0] - re[half]
-    for k in range(1, quarter + 1):
-        if 2 * k == half:
-            even_re[k], odd_re[k] = re[k], -im[k]
+    one_re, one_im = [None] * (eighth + 1), [None] * (eighth + 1)
+    three_re, three_im = [None] * (eighth + 1), [None] * (eighth + 1)
+    even_re[0], total = re[0] + re[half], re[0] - re[half]
+    even_re[quarter] = re[quarter]
+    one_re[0], three_re[0] = total - im[quarter], total + im[quarter]
+    for k in range(1, eighth + 1):
+        sum_re, even_re[k] = re[k] - re[half - k], re[k] + re[half - k]
+        sum_im, even_im[k] = im[k] + im[half - k], im[k] - im[half - k]
+        if 2 * k == quarter:
+            c = math.sqrt(0.5)
+            one_re[k], three_re[k] = c * (sum_re - sum_im), -c * (sum_re + sum_im)
             continue
-        c, s = math.cos(2 * math.pi * k / n), -math.sin(2 * math.pi * k / n)
-        even_re[k], even_im[k] = re[k] + re[half - k], im[k] - im[half - k]
-        a, b = re[k] - re[half - k], im[k] + im[half - k]
-        if 8 * k == n:
-            odd_re[k], odd_im[k] = c * (a - b), c * (a + b)
-        else:
-            odd_re[k], odd_im[k] = c * a + s * b, c * b - s * a
+        mirror = quarter - k
+        even_re[mirror], gap_im = re[quarter + k] + re[mirror], re[quarter + k] - re[mirror]
+        even_im[mirror] = im[mirror] - im[quarter + k]
+        gap_re = -(im[quarter + k] + im[mirror])
+        one = sum_re + gap_re, sum_im + gap_im
+        three = sum_re - gap_re, sum_im - gap_im
+        one_re[k], one_im[k] = turned_by(n, -k, *one)
+        three_re[k], three_im[k] = turned_by(n, -3 * k, *three)
     values = [None] * n
-    values[0::2] = real_dft_transposed(even_re[: quarter + 1], even_im[: quarter + 1])
-    values[1::2] = real_dft_transposed(odd_re[: quarter + 1], odd_im[: quarter + 1])
+    values[0::2] = real_dft_transposed(even_re, even_im)
+    values[1::4] = real_dft_transposed(one_re, one_im)
+    values[3::4] = real_dft_transposed(three_re, three_im)
     return values
 
 
@@ -90,7 +114,7 @@
 def kernel(
     tn, pn, t_hbm, psi_hbm, weights_hbm, table_hbm, occupied_ref, retained_ref, out_ref,
     planes, psi_ref, weights_ref, table_ref, spec, part, pair_buf, rs_buf, t_buf, a_buf,
-    gram_ref, g_buf, inv_ref,
+    gram_ref, g_col, g_buf, inv_ref,
 ):
     slab = planes.shape[0] // pn
     rows = planes.shape[1]
@@ -99,20 +123,20 @@
         functools.partial(
             exchange, tn, pn, t_hbm, psi_hbm, weights_hbm, table_hbm, occupied_ref, retained_ref,
             out_ref, planes, psi_ref, weights_ref, table_ref, spec, part, pair_buf, rs_buf, t_buf,
-            a_buf, gram_ref, g_buf, inv_ref,
+            a_buf, gram_ref, g_col, g_buf, inv_ref,
         ),
         dma((2, rows)), dma((4,)), dma((pn // 2, slab)), dma((pn // 2, slab)),
         dma((pn // 2, slab)), dma((pn // 2, slab)), dma((tn,)), dma((tn,)),
-        dma((tn, tn, slab)), dma((tn, slab)), dma((tn,)), dma((tn,)),
+        dma((tn, tn, slab)), dma((tn, slab)), dma((tn,)), dma((tn,)), dma, dma,
     )
 
 
 def exchange(
     tn, pn, t_hbm, psi_hbm, weights_hbm, table_hbm, occupied_ref, retained_ref, out_ref,
     planes, psi_ref, weights_ref, table_ref, spec, part, pair_buf, rs_buf, t_buf, a_buf,
-    gram_ref, g_buf, inv_ref,
+    gram_ref, g_col, g_buf, inv_ref,
     plane_sem, load_sem, pair_send, pair_recv, rs_send, rs_recv, t_send, t_recv,
-    a_send, a_recv, g_send, g_recv,
+    a_send, a_recv, g_send, g_recv, share_send, share_recv,
 ):
     t, p = lax.axis_index("tgt"), lax.axis_index("ptr")
     length, rows, cells = planes.shape
@@ -122,7 +146,6 @@
     all_cells = length * cells
     total_rows = tn * rows
     width = inv_ref.shape[1]
-    me = t * pn + p
     chips = pn // 2
     chip, core = p // 2, lax.rem(p, 2)
     partner = p + 1 - 2 * core
@@ -148,11 +171,15 @@
 
     barrier = pltpu.get_barrier_semaphore()
     for tt in range(tn):
-        for pp in range(pn):
-
-            @pl.when((t != tt) | (p != pp))
-            def greet():
-                pl.semaphore_signal(barrier, inc=1, device_id=(tt, pp), device_id_type=MESH)
+
+        @pl.when(t != tt)
+        def column():
+            pl.semaphore_signal(barrier, inc=1, device_id=(tt, p), device_id_type=MESH)
+
+    for d in range(1, pn):
+        pl.semaphore_signal(
+            barrier, inc=1, device_id=(t, lax.rem(p + d, pn)), device_id_type=MESH
+        )
 
     def pair_copy(q, r):
         return pltpu.make_async_remote_copy(
@@ -236,35 +263,43 @@
     def sent(copy):
         copy.wait_send()
 
-    def g_copy(target, q):
-        return pltpu.make_async_remote_copy(
-            src_ref=g_buf.at[me], dst_ref=g_buf.at[me],
-            send_sem=g_send.at[target], recv_sem=g_recv.at[t],
-            device_id=(target, q), device_id_type=MESH,
-        )
-
-    def g_all(s, count):
-        every = g_buf.at[pl.ds(s * pn, count)]
-        return pltpu.make_async_remote_copy(
-            src_ref=every, dst_ref=every, send_sem=g_send.at[s], recv_sem=g_recv.at[s],
+    def g_up(source, target):
+        return pltpu.make_async_remote_copy(
+            src_ref=g_col.at[source], dst_ref=g_col.at[source],
+            send_sem=g_send.at[target], recv_sem=g_recv.at[source],
+            device_id=(target, p), device_id_type=MESH,
+        )
+
+    def g_share(d):
+        return pltpu.make_async_remote_copy(
+            src_ref=g_col, dst_ref=g_buf.at[p],
+            send_sem=share_send, recv_sem=share_recv,
+            device_id=(t, lax.rem(p + d, pn)), device_id_type=MESH,
+        )
+
+    def g_shares():
+        every = g_buf.at[pl.ds(0, pn - 1)]
+        return pltpu.make_async_remote_copy(
+            src_ref=every, dst_ref=every, send_sem=share_send, recv_sem=share_recv,
             device_id=(t, partner), device_id_type=MESH,
         )
 
     group_of = lax.broadcasted_iota(jnp.int32, (rows, lanes), 1) // length
-    at_group = [group_of == g for g in range(groups)]
     per_block = groups // occupied_ref.shape[0]
-    occ = 0.25 + 0.75 * occupied_ref[0].astype(jnp.float32) * jnp.ones((rows, lanes), jnp.float32)
+    lane_group = lax.broadcasted_iota(jnp.int32, (length, lanes), 1) // length
+    occ = 0.25 + 0.75 * occupied_ref[0].astype(jnp.float32) * jnp.ones((length, lanes), jnp.float32)
     for i in range(1, occupied_ref.shape[0]):
         level = 0.25 + 0.75 * occupied_ref[i].astype(jnp.float32)
-        occ = jnp.where(group_of >= i * per_block, level, occ)
-
+        occ = jnp.where(lane_group >= i * per_block, level, occ)
+
+    at_group = [group_of == g for g in range(groups)]
     def pick(options):
         chosen = options[0]
         for g in range(1, groups):
             chosen = jnp.where(at_group[g], options[g], chosen)
         return chosen
 
-    def rolled(value, steps):
+    def turn(value, steps):
         steps = steps % groups
         return value if steps == 0 else pltpu.roll(value, steps * length, 1)
 
@@ -288,7 +323,7 @@
             x = i * FORWARD + j
             for q in range(length // groups):
                 v = planes[x, :, q * lanes : (q + 1) * lanes]
-                turned = [rolled(v, s) for s in range(groups)]
+                turned = [turn(v, s) for s in range(groups)]
                 for g in range(groups):
                     y = q * groups + g
                     spread = pick([turned[(h - g) % groups] for h in range(groups)])
@@ -301,15 +336,18 @@
                 spec[i * FORWARD + j, m] = modes[m]
 
     t_buf[t] = planes[pl.ds(p * slab, slab)]
+    for x in range(length):
+        psi_ref[x] = psi_ref[x] * occ
     for s in range(1, tn):
 
         @pl.when(s > t)
         def clear():
             a_buf[s] = jnp.zeros(a_buf.shape[1:], jnp.float32)
+            g_col[s] = jnp.zeros(g_col.shape[1:], jnp.float32)
 
     gram_ref[...] = jnp.zeros_like(gram_ref)
     table_load.wait()
-    pl.semaphore_wait(barrier, tn * pn - 1)
+    pl.semaphore_wait(barrier, tn + pn - 2)
     t_sends(start)
 
     @pl.loop(0, length)
@@ -350,8 +388,7 @@
                     terms.append(potential[y * rows : (y + 1) * rows] * psi_ref[x, y : y + 1, :])
                 total = None
                 for s in range(groups):
-                    chosen = pick([terms[(h - s) % groups] for h in range(groups)])
-                    moved = rolled(chosen * occ, -s)
+                    moved = turn(pick([terms[(h - s) % groups] for h in range(groups)]), -s)
                     total = moved if total is None else total + moved
                 part[x, :, q * lanes : (q + 1) * lanes] = total
 
@@ -381,30 +418,40 @@
             rs_copy(c, c, r).wait_recv()
             own = own + rs_buf[c, r]
         a_buf[t, r] = own
-        a_route(r, start)
+
+        @pl.when(r < slab - HELD)
+        def at_once():
+            a_route(r, start)
+
         every = jnp.concatenate([t_buf[s, r] for s in range(tn)], axis=0)
         gram_ref[...] += lax.dot_general(
             own, every, (((1,), (1,)), ((), ())),
             precision=HIGHEST, preferred_element_type=jnp.float32,
         )
 
-        @pl.when(r > 0)
-        def earlier():
-            a_onward(r - 1, start, True)
-
     gram = gram_ref[...] * (1.0 / all_cells)
     fold = 128 // total_rows
     short = rows // fold
-    g_buf[me] = jnp.concatenate([gram[i * short : (i + 1) * short] for i in range(fold)], axis=1)
-
-    for target in reversed(range(tn)):
-        for q in range(pn):
-
-            @pl.when((t < target) | ((t == target) & (p != q)))
-            def spread():
-                g_copy(target, q).start()
-
-    a_onward(slab - 1, start, True)
+    g_col[t] = jnp.concatenate([gram[i * short : (i + 1) * short] for i in range(fold)], axis=1)
+    for target in reversed(range(1, tn)):
+
+        @pl.when(t < target)
+        def upward():
+            g_up(t, target).start()
+
+    for r in range(slab - HELD):
+        a_onward(r, start, True)
+    for r in range(slab - HELD, slab):
+        a_route(r, start)
+    for s in range(tn - 1):
+
+        @pl.when(t > s)
+        def below():
+            g_up(s, t).wait_recv()
+
+    for d in range(1, pn):
+        g_share(d).start()
+    g_buf[p] = g_col[...]
     t_sends(sent)
 
     @pl.loop(0, slab)
@@ -414,22 +461,15 @@
         for d in range(1, chips):
             rs_copy(lax.rem(chip + d, chips), chip, r).wait_send()
 
+    for r in range(slab - HELD, slab):
+        a_onward(r, start, True)
+    g_shares().wait_recv()
+    blocks = []
+    summed = g_buf[0]
+    for q in range(1, pn):
+        summed = summed + g_buf[q]
     for s in range(tn):
-
-        @pl.when(t > s)
-        def others():
-            g_all(s, pn).wait_recv()
-
-        @pl.when(t == s)
-        def mates():
-            g_all(s, pn - 1).wait_recv()
-
-    blocks = []
-    for s in range(tn):
-        block = g_buf[s * pn]
-        for q in range(1, pn):
-            block = block + g_buf[s * pn + q]
-        blocks += [block[:, i * total_rows : (i + 1) * total_rows] for i in range(fold)]
+        blocks += [summed[s, :, i * total_rows : (i + 1) * total_rows] for i in range(fold)]
     square = jnp.concatenate(blocks, axis=0)
     square = jnp.concatenate(
         [square, jnp.zeros((total_rows, width - total_rows), jnp.float32)], axis=1
@@ -476,16 +516,13 @@
             mine, every, precision=HIGHEST, preferred_element_type=jnp.float32
         )
 
-    for target in range(tn):
+    for target in range(1, tn):
 
         @pl.when(t < target)
-        def upward():
-            g_all(target, pn).wait_send()
-
-        @pl.when(t == target)
-        def within():
-            g_all(target, pn - 1).wait_send()
-
+        def ended():
+            g_up(t, target).wait_send()
+
+    g_shares().wait_send()
     for r in range(slab):
         a_route(r, sent)
         a_onward(r, sent, False)
@@ -535,14 +572,15 @@
             pltpu.VMEM(partners.shape, jnp.float32),
             pltpu.VMEM(weights.shape, weights.dtype),
             pltpu.VMEM(table.shape, jnp.float32),
-            pltpu.VMEM((length, length, rows, lanes), jnp.float32),
+            pltpu.VMEM((length, length + 1, rows, lanes), jnp.float32),
             planes,
             received,
             received,
             block,
             block,
             pltpu.VMEM((rows, total_rows), jnp.float32),
-            pltpu.VMEM((tn * pn, rows * total_rows // 128, 128), jnp.float32),
+            pltpu.VMEM((tn, rows * total_rows // 128, 128), jnp.float32),
+            pltpu.VMEM((pn, tn, rows * total_rows // 128, 128), jnp.float32),
             pltpu.VMEM((total_rows, width), jnp.float32),
         ],
         compiler_params=pltpu.CompilerParams(collective_id=0, has_side_effects=True),

time: 28.7 us -> 26.9 us (0.937)
  Pallas kernels: 26.1 us -> 24.6 us
    pallas_call x1, Pallas kernels: 26.1 us -> 24.6 us  [shards(): pl.pallas_call(functools.partial(kernel, tn, pn), out_shape=pltpu.VMEM((r...]
where the time goes in v2:
time: 26.9 us; the launch traced here: 26.6 us
  Pallas kernels  24.6 us (91%)
  between operations  1.3 us (5%)
  local copies, waits for them, and re-layouts  0.66 us (2%)
    pallas_call x1, Pallas kernels, shards(): pl.pallas_call(functools.partial(kernel, tn, pn), out_shape=pltpu.VMEM((r...  24.6 us
    unnamed x1, local copies, waits for them, and re-layouts  0.66 us

profile of v2, /device:TPU:25, one launch (start us, length us, event | category | flops | bytes accessed | tf_op | source)
XLA Modules:
  0.0 26.6 jit_solution(2626692593650455040)
XLA Ops:
  1.3 24.6 %exchange.1 = f32[8,4,1024]{2,1,0:T(4,128)S(1)} custom-call(f32[8,32,1024]{2,1,0:T(8,128)} %t_hbm.1, f32[32,32,128]{2,1,0:T(8,128)} %psi_hbm.1, bf16[256,256]{1,0:T(8,128)(2,1)} %constant.4.clone.weights_hbm, f32[32,17,128]{2,1,0:T(8,128)} %constant.5.clone.table_hbm, s32[1]{0:T(128)S(6)} %copy.9.occupied_ref, s32[1]{0:T(128)S(6)} %copy.10.retained_ref), custom_call_target="tpu_custom_call" | custom-call | tf_op jit(solution)/shard_map/exchange/pallas_call | solution.py:565
  25.9 0.7 %copy.8 = f32[8,4,1024]{2,1,0:T(4,128)} copy(f32[8,4,1024]{2,1,0:T(4,128)S(1)} %exchange.1) | data formatting | bytes 262144

commit v3 on v2

--- a/solution.py
+++ b/solution.py
@@ -13,7 +13,8 @@
 MESH = pl.DeviceIdType.MESH
 FORWARD = 8
 BACKWARD = 4
-PIVOTS = 4
+PIVOTS = 8
+MIDDLE = 2
 HELD = 2
 
 
@@ -245,7 +246,7 @@
                 for target in range(s + 2, tn):
                     act(a_copy(s, target, r))
 
-    def a_arrivals():
+    def a_arrivals(r):
         for s in range(tn - 1):
             if s % 2 == 1 and s + 2 < tn:
                 here = t > s + 1
@@ -254,8 +255,7 @@
 
             @pl.when(here)
             def arrived():
-                for r in range(slab):
-                    a_copy(s, s + 1, r).wait_recv()
+                a_copy(s, s + 1, r).wait_recv()
 
     def start(copy):
         copy.start()
@@ -350,17 +350,19 @@
     pl.semaphore_wait(barrier, tn + pn - 2)
     t_sends(start)
 
-    @pl.loop(0, length)
-    def middle(m):
-        modes = flat_dft([spec[x, m] for x in range(length)])
+    @pl.loop(0, length // MIDDLE)
+    def middle(step):
         half = length // 2
-        scaled = []
-        for i in range(length):
-            k = i if i <= half else i - half
-            scaled.append(modes[i] * table_ref[m, k : k + 1, :])
-        values = flat_dft_transposed(scaled)
-        for x in range(length):
-            spec[x, m] = values[x]
+        for j in range(MIDDLE):
+            m = step * MIDDLE + j
+            modes = flat_dft([spec[x, m] for x in range(length)])
+            scaled = []
+            for i in range(length):
+                k = i if i <= half else i - half
+                scaled.append(modes[i] * table_ref[m, k : k + 1, :])
+            values = flat_dft_transposed(scaled)
+            for x in range(length):
+                spec[x, m] = values[x]
 
     per = chips // BACKWARD
 
@@ -408,7 +410,12 @@
                     part[x] = part[x] + pair_buf[owner // 2, r]
                     rs_copy(owner // 2, chip, r).start()
 
-    t_arrivals()
+    def add_gram(r):
+        every = jnp.concatenate([t_buf[s, r] for s in range(tn)], axis=0)
+        gram_ref[...] += lax.dot_general(
+            a_buf[t, r], every, (((1,), (1,)), ((), ())),
+            precision=HIGHEST, preferred_element_type=jnp.float32,
+        )
 
     @pl.loop(0, slab)
     def reduce(r):
@@ -423,12 +430,15 @@
         def at_once():
             a_route(r, start)
 
-        every = jnp.concatenate([t_buf[s, r] for s in range(tn)], axis=0)
-        gram_ref[...] += lax.dot_general(
-            own, every, (((1,), (1,)), ((), ())),
-            precision=HIGHEST, preferred_element_type=jnp.float32,
-        )
-
+        @pl.when(r == 1)
+        def met():
+            t_arrivals()
+
+        @pl.when(r > 0)
+        def earlier():
+            add_gram(r - 1)
+
+    add_gram(slab - 1)
     gram = gram_ref[...] * (1.0 / all_cells)
     fold = 128 // total_rows
     short = rows // fold
@@ -509,8 +519,8 @@
     keeping = (row_of < retained_ref[0]).astype(jnp.float32)
     inv_ref[...] = work * scale * keeping
     mine = inv_ref[pl.ds(pl.multiple_of(t * rows, rows), rows), :][:, total_rows : 2 * total_rows]
-    a_arrivals()
     for x in range(slab):
+        a_arrivals(x)
         every = jnp.concatenate([a_buf[s, x] for s in range(tn)], axis=0)
         out_ref[:, x, :] = jnp.dot(
             mine, every, precision=HIGHEST, preferred_element_type=jnp.float32

time: 26.9 us -> 26.2 us (0.974)
  the two profiles are of different devices: /device:TPU:25 before, /device:TPU:24 now
where the time goes in v3:
time: 26.2 us; the launch traced here: 26 us
  Pallas kernels  24 us (92%)
  between operations  1.3 us (5%)
  local copies, waits for them, and re-layouts  0.66 us (3%)
    pallas_call x1, Pallas kernels, shards(): pl.pallas_call(functools.partial(kernel, tn, pn), out_shape=pltpu.VMEM((r...  24 us
    unnamed x1, local copies, waits for them, and re-layouts  0.66 us

profile of v3, /device:TPU:24, one launch (start us, length us, event | category | flops | bytes accessed | tf_op | source)
XLA Modules:
  0.0 26.0 jit_solution(9102313896997289556)
XLA Ops:
  1.3 24.0 %exchange.1 = f32[8,4,1024]{2,1,0:T(4,128)S(1)} custom-call(f32[8,32,1024]{2,1,0:T(8,128)} %t_hbm.1, f32[32,32,128]{2,1,0:T(8,128)} %psi_hbm.1, bf16[256,256]{1,0:T(8,128)(2,1)} %constant.4.clone.weights_hbm, f32[32,17,128]{2,1,0:T(8,128)} %constant.5.clone.table_hbm, s32[1]{0:T(128)S(6)} %copy.9.occupied_ref, s32[1]{0:T(128)S(6)} %copy.10.retained_ref), custom_call_target="tpu_custom_call" | custom-call | tf_op jit(solution)/shard_map/exchange/pallas_call | solution.py:575
  25.3 0.7 %copy.8 = f32[8,4,1024]{2,1,0:T(4,128)} copy(f32[8,4,1024]{2,1,0:T(4,128)S(1)} %exchange.1) | data formatting | bytes 262144

commit v4 on v3

--- a/solution.py
+++ b/solution.py
@@ -227,7 +227,7 @@
             device_id=(target, p), device_id_type=MESH,
         )
 
-    def a_route(r, act):
+    def a_route(r, act, straight):
         for s in range(tn - 1):
             for target in range(s + 1, tn):
                 if s % 2 == 0 or target == s + 1:
@@ -236,10 +236,16 @@
                     def direct():
                         act(a_copy(s, target, r))
 
-    def a_onward(r, act, wait):
+                elif straight:
+
+                    @pl.when((t == s) & (core >= 0))
+                    def far():
+                        act(a_copy(s, target, r))
+
+    def a_onward(r, act, wait, straight):
         for s in range(1, tn - 2, 2):
 
-            @pl.when(t == s + 1)
+            @pl.when((t == s + 1) & ((core < 0) if straight else True))
             def onward():
                 if wait:
                     a_copy(s, s + 1, r).wait_recv()
@@ -247,11 +253,11 @@
                     act(a_copy(s, target, r))
 
     def a_arrivals(r):
+        straight = r >= slab - HELD
         for s in range(tn - 1):
+            here = t > s
             if s % 2 == 1 and s + 2 < tn:
-                here = t > s + 1
-            else:
-                here = t > s
+                here = (t > s + 1) | ((t == s + 1) & (core >= 0)) if straight else t > s + 1
 
             @pl.when(here)
             def arrived():
@@ -428,7 +434,7 @@
 
         @pl.when(r < slab - HELD)
         def at_once():
-            a_route(r, start)
+            a_route(r, start, False)
 
         @pl.when(r == 1)
         def met():
@@ -450,9 +456,9 @@
             g_up(t, target).start()
 
     for r in range(slab - HELD):
-        a_onward(r, start, True)
+        a_onward(r, start, True, False)
     for r in range(slab - HELD, slab):
-        a_route(r, start)
+        a_route(r, start, True)
     for s in range(tn - 1):
 
         @pl.when(t > s)
@@ -472,7 +478,7 @@
             rs_copy(lax.rem(chip + d, chips), chip, r).wait_send()
 
     for r in range(slab - HELD, slab):
-        a_onward(r, start, True)
+        a_onward(r, start, True, True)
     g_shares().wait_recv()
     blocks = []
     summed = g_buf[0]
@@ -497,27 +503,36 @@
     symmetric = jnp.where(apart == 0, 0.5 * both, both)
     unit = (lane_of == row_of + total_rows) | ((lane_of == row_of) & (row_block > t))
     work = jnp.where(unit, 1.0, symmetric)
-    scale = jnp.zeros((total_rows, width), jnp.float32)
-    for k in range(0, total_rows, PIVOTS):
+    line_of = lax.broadcasted_iota(jnp.int32, (PIVOTS, width), 0)
+    strips = [work[k : k + PIVOTS, :] for k in range(0, total_rows, PIVOTS)]
+    for k, strip in enumerate(strips):
+        lines = [jnp.broadcast_to(strip[i : i + 1, :], strip.shape) for i in range(PIVOTS)]
+        lane = [k * PIVOTS + i for i in range(PIVOTS)]
+        corner = [
+            [jnp.broadcast_to(line[:, h : h + 1], line.shape) for h in lane] for line in lines
+        ]
+        below = range(k + 1, len(strips))
         columns = [
-            jnp.broadcast_to(work[:, k + i : k + i + 1], (total_rows, width)) for i in range(PIVOTS)
+            [jnp.broadcast_to(strips[g][:, h : h + 1], strip.shape) for g in below] for h in lane
         ]
-        lines = [work[k + i : k + i + 1, :] for i in range(PIVOTS)]
-        corner = [[columns[j][k + i : k + i + 1, :] for j in range(PIVOTS)] for i in range(PIVOTS)]
+        done = strip
         for i in range(PIVOTS):
             pivot = corner[i][i]
-            scale = jnp.where(row_of == k + i, 1.0 / jnp.sqrt(pivot), scale)
             inverse = 1.0 / pivot
             scaled = lines[i] * inverse
+            done = jnp.where(line_of == i, lines[i] * (1.0 / jnp.sqrt(pivot)), done)
             for m in range(i + 1, PIVOTS):
                 factor = corner[i][m] * inverse
-                columns[m] = columns[m] - columns[i] * factor
-                lines[m] = lines[m] - corner[m][i] * scaled
-                for h in range(i + 1, PIVOTS):
-                    corner[h][m] = corner[h][m] - corner[h][i] * factor
-            work = work - jnp.where(row_of > k + i, columns[i], 0.0) * scaled
+                lines[m] = lines[m] - corner[i][m] * scaled
+                for h in range(m, PIVOTS):
+                    corner[m][h] = corner[m][h] - factor * corner[i][h]
+                columns[m] = [c - d * factor for c, d in zip(columns[m], columns[i])]
+            for g, column in zip(below, columns[i]):
+                strips[g] = strips[g] - column * scaled
+        strips[k] = done
+    work = jnp.concatenate(strips, axis=0)
     keeping = (row_of < retained_ref[0]).astype(jnp.float32)
-    inv_ref[...] = work * scale * keeping
+    inv_ref[...] = work * keeping
     mine = inv_ref[pl.ds(pl.multiple_of(t * rows, rows), rows), :][:, total_rows : 2 * total_rows]
     for x in range(slab):
         a_arrivals(x)
@@ -534,8 +549,8 @@
 
     g_shares().wait_send()
     for r in range(slab):
-        a_route(r, sent)
-        a_onward(r, sent, False)
+        a_route(r, sent, r >= slab - HELD)
+        a_onward(r, sent, False, r >= slab - HELD)
 
 
 def constants(length, groups):

time: 26.2 us -> 25.6 us (0.977)
  the two profiles are of different devices: /device:TPU:24 before, /device:TPU:25 now
where the time goes in v4:
time: 25.6 us; the launch traced here: 25.4 us
  Pallas kernels  23.4 us (91%)
  between operations  1.3 us (5%)
  local copies, waits for them, and re-layouts  0.66 us (3%)
    pallas_call x1, Pallas kernels, shards(): pl.pallas_call(functools.partial(kernel, tn, pn), out_shape=pltpu.VMEM((r...  23.4 us
    unnamed x1, local copies, waits for them, and re-layouts  0.66 us

profile of v4, /device:TPU:25, one launch (start us, length us, event | category | flops | bytes accessed | tf_op | source)
XLA Modules:
  0.0 25.4 jit_solution(515579019642112275)
XLA Ops:
  1.3 23.4 %exchange.1 = f32[8,4,1024]{2,1,0:T(4,128)S(1)} custom-call(f32[8,32,1024]{2,1,0:T(8,128)} %t_hbm.1, f32[32,32,128]{2,1,0:T(8,128)} %psi_hbm.1, bf16[256,256]{1,0:T(8,128)(2,1)} %constant.4.clone.weights_hbm, f32[32,17,128]{2,1,0:T(8,128)} %constant.5.clone.table_hbm, s32[1]{0:T(128)S(6)} %copy.9.occupied_ref, s32[1]{0:T(128)S(6)} %copy.10.retained_ref), custom_call_target="tpu_custom_call" | custom-call | tf_op jit(solution)/shard_map/exchange/pallas_call | solution.py:590
  24.7 0.7 %copy.8 = f32[8,4,1024]{2,1,0:T(4,128)} copy(f32[8,4,1024]{2,1,0:T(4,128)S(1)} %exchange.1) | data formatting | bytes 262144

commit v5 on v4

--- a/solution.py
+++ b/solution.py
@@ -341,17 +341,8 @@
             for m in range(length):
                 spec[i * FORWARD + j, m] = modes[m]
 
-    t_buf[t] = planes[pl.ds(p * slab, slab)]
     for x in range(length):
         psi_ref[x] = psi_ref[x] * occ
-    for s in range(1, tn):
-
-        @pl.when(s > t)
-        def clear():
-            a_buf[s] = jnp.zeros(a_buf.shape[1:], jnp.float32)
-            g_col[s] = jnp.zeros(g_col.shape[1:], jnp.float32)
-
-    gram_ref[...] = jnp.zeros_like(gram_ref)
     table_load.wait()
     pl.semaphore_wait(barrier, tn + pn - 2)
     t_sends(start)
@@ -381,7 +372,11 @@
         away = (i == 0) | ((odd == 1) & jnp.logical_not(last))
         r = jnp.where(away, (i + 1) // 2, jnp.where(last, slab - 1, i // 2 - 1))
         side = jnp.where(away, 1 - core, core)
-        owners = [2 * lax.rem(chip + 1 + first + j, chips) + side for j in range(BACKWARD)]
+        if chips == BACKWARD == 4:
+            order = [chips - 1 - chip, lax.rem(chip + 2, chips), chip + 1 - 2 * lax.rem(chip, 2), chip]
+        else:
+            order = [lax.rem(chip + 1 + first + j, chips) for j in range(BACKWARD)]
+        owners = [2 * c + side for c in order]
         values = []
         for q in owners:
             values += flat_dft_transposed([spec[q * slab + r, m] for m in range(length)])
@@ -416,6 +411,15 @@
                     part[x] = part[x] + pair_buf[owner // 2, r]
                     rs_copy(owner // 2, chip, r).start()
 
+    t_buf[t] = planes[pl.ds(p * slab, slab)]
+    for s in range(1, tn):
+
+        @pl.when(s > t)
+        def clear():
+            a_buf[s] = jnp.zeros(a_buf.shape[1:], jnp.float32)
+            g_col[s] = jnp.zeros(g_col.shape[1:], jnp.float32)
+
+    gram_ref[...] = jnp.zeros_like(gram_ref)
     def add_gram(r):
         every = jnp.concatenate([t_buf[s, r] for s in range(tn)], axis=0)
         gram_ref[...] += lax.dot_general(
@@ -479,6 +483,15 @@
 
     for r in range(slab - HELD, slab):
         a_onward(r, start, True, True)
+    for target in range(1, tn):
+
+        @pl.when(t < target)
+        def ended():
+            g_up(t, target).wait_send()
+
+    for r in range(slab - HELD):
+        a_route(r, sent, False)
+        a_onward(r, sent, False, False)
     g_shares().wait_recv()
     blocks = []
     summed = g_buf[0]
@@ -541,16 +554,10 @@
             mine, every, precision=HIGHEST, preferred_element_type=jnp.float32
         )
 
-    for target in range(1, tn):
-
-        @pl.when(t < target)
-        def ended():
-            g_up(t, target).wait_send()
-
     g_shares().wait_send()
-    for r in range(slab):
-        a_route(r, sent, r >= slab - HELD)
-        a_onward(r, sent, False, r >= slab - HELD)
+    for r in range(slab - HELD, slab):
+        a_route(r, sent, True)
+        a_onward(r, sent, False, True)
 
 
 def constants(length, groups):

time: 25.6 us -> 25.5 us (level)
  no operation moved by 1% of the time
where the time goes in v5:
time: 25.5 us; the launch traced here: 25.3 us
  Pallas kernels  23.3 us (91%)
  between operations  1.3 us (5%)
  local copies, waits for them, and re-layouts  0.66 us (3%)
    pallas_call x1, Pallas kernels, shards(): pl.pallas_call(functools.partial(kernel, tn, pn), out_shape=pltpu.VMEM((r...  23.3 us
    unnamed x1, local copies, waits for them, and re-layouts  0.66 us

profile of v5, /device:TPU:25, one launch (start us, length us, event | category | flops | bytes accessed | tf_op | source)
XLA Modules:
  0.0 25.3 jit_solution(15102186535440417648)
XLA Ops:
  1.3 23.3 %exchange.1 = f32[8,4,1024]{2,1,0:T(4,128)S(1)} custom-call(f32[8,32,1024]{2,1,0:T(8,128)} %t_hbm.1, f32[32,32,128]{2,1,0:T(8,128)} %psi_hbm.1, bf16[256,256]{1,0:T(8,128)(2,1)} %constant.4.clone.weights_hbm, f32[32,17,128]{2,1,0:T(8,128)} %constant.5.clone.table_hbm, s32[1]{0:T(128)S(6)} %copy.9.occupied_ref, s32[1]{0:T(128)S(6)} %copy.10.retained_ref), custom_call_target="tpu_custom_call" | custom-call | tf_op jit(solution)/shard_map/exchange/pallas_call | solution.py:597
  24.6 0.7 %copy.8 = f32[8,4,1024]{2,1,0:T(4,128)} copy(f32[8,4,1024]{2,1,0:T(4,128)S(1)} %exchange.1) | data formatting | bytes 262144

commit v6 on v5

--- a/solution.py
+++ b/solution.py
@@ -463,15 +463,6 @@
         a_onward(r, start, True, False)
     for r in range(slab - HELD, slab):
         a_route(r, start, True)
-    for s in range(tn - 1):
-
-        @pl.when(t > s)
-        def below():
-            g_up(s, t).wait_recv()
-
-    for d in range(1, pn):
-        g_share(d).start()
-    g_buf[p] = g_col[...]
     t_sends(sent)
 
     @pl.loop(0, slab)
@@ -483,6 +474,16 @@
 
     for r in range(slab - HELD, slab):
         a_onward(r, start, True, True)
+
+    for s in range(tn - 1):
+
+        @pl.when(t > s)
+        def below():
+            g_up(s, t).wait_recv()
+
+    for d in range(1, pn):
+        g_share(d).start()
+    g_buf[p] = g_col[...]
     for target in range(1, tn):
 
         @pl.when(t < target)

time: 25.5 us -> 25.5 us (level)
  no operation moved by 1% of the time
where the time goes in v6:
time: 25.5 us; the launch traced here: 25.3 us
  Pallas kernels  23.3 us (91%)
  between operations  1.3 us (5%)
  local copies, waits for them, and re-layouts  0.66 us (3%)
    pallas_call x1, Pallas kernels, shards(): pl.pallas_call(functools.partial(kernel, tn, pn), out_shape=pltpu.VMEM((r...  23.3 us
    unnamed x1, local copies, waits for them, and re-layouts  0.66 us

profile of v6, /device:TPU:25, one launch (start us, length us, event | category | flops | bytes accessed | tf_op | source)
XLA Modules:
  0.0 25.3 jit_solution(16749406054802224137)
XLA Ops:
  1.3 23.3 %exchange.1 = f32[8,4,1024]{2,1,0:T(4,128)S(1)} custom-call(f32[8,32,1024]{2,1,0:T(8,128)} %t_hbm.1, f32[32,32,128]{2,1,0:T(8,128)} %psi_hbm.1, bf16[256,256]{1,0:T(8,128)(2,1)} %constant.4.clone.weights_hbm, f32[32,17,128]{2,1,0:T(8,128)} %constant.5.clone.table_hbm, s32[1]{0:T(128)S(6)} %copy.9.occupied_ref, s32[1]{0:T(128)S(6)} %copy.10.retained_ref), custom_call_target="tpu_custom_call" | custom-call | tf_op jit(solution)/shard_map/exchange/pallas_call | solution.py:598
  24.6 0.7 %copy.8 = f32[8,4,1024]{2,1,0:T(4,128)} copy(f32[8,4,1024]{2,1,0:T(4,128)S(1)} %exchange.1) | data formatting | bytes 262144

commit v7 on v6

--- a/solution.py
+++ b/solution.py
@@ -16,6 +16,7 @@
 PIVOTS = 8
 MIDDLE = 2
 HELD = 2
+NEAR = 2
 
 
 def turned_by(n, k, re, im):
@@ -115,7 +116,7 @@
 def kernel(
     tn, pn, t_hbm, psi_hbm, weights_hbm, table_hbm, occupied_ref, retained_ref, out_ref,
     planes, psi_ref, weights_ref, table_ref, spec, part, pair_buf, rs_buf, t_buf, a_buf,
-    gram_ref, g_col, g_buf, inv_ref,
+    gram_ref, g_col, g_near, g_buf, inv_ref,
 ):
     slab = planes.shape[0] // pn
     rows = planes.shape[1]
@@ -124,20 +125,21 @@
         functools.partial(
             exchange, tn, pn, t_hbm, psi_hbm, weights_hbm, table_hbm, occupied_ref, retained_ref,
             out_ref, planes, psi_ref, weights_ref, table_ref, spec, part, pair_buf, rs_buf, t_buf,
-            a_buf, gram_ref, g_col, g_buf, inv_ref,
+            a_buf, gram_ref, g_col, g_near, g_buf, inv_ref,
         ),
         dma((2, rows)), dma((4,)), dma((pn // 2, slab)), dma((pn // 2, slab)),
         dma((pn // 2, slab)), dma((pn // 2, slab)), dma((tn,)), dma((tn,)),
-        dma((tn, tn, slab)), dma((tn, slab)), dma((tn,)), dma((tn,)), dma, dma,
+        dma((tn, tn, slab)), dma((tn, slab)), dma((tn,)), dma((tn,)), dma, dma, dma((NEAR,)), dma((NEAR,)),
     )
 
 
 def exchange(
     tn, pn, t_hbm, psi_hbm, weights_hbm, table_hbm, occupied_ref, retained_ref, out_ref,
     planes, psi_ref, weights_ref, table_ref, spec, part, pair_buf, rs_buf, t_buf, a_buf,
-    gram_ref, g_col, g_buf, inv_ref,
+    gram_ref, g_col, g_near, g_buf, inv_ref,
     plane_sem, load_sem, pair_send, pair_recv, rs_send, rs_recv, t_send, t_recv,
     a_send, a_recv, g_send, g_recv, share_send, share_recv,
+    near_send, near_recv,
 ):
     t, p = lax.axis_index("tgt"), lax.axis_index("ptr")
     length, rows, cells = planes.shape
@@ -182,6 +184,15 @@
             barrier, inc=1, device_id=(t, lax.rem(p + d, pn)), device_id_type=MESH
         )
 
+    for k in range(1, NEAR + 1):
+
+        @pl.when(t >= k)
+        def senders():
+            for d in range(1, pn):
+                pl.semaphore_signal(
+                    barrier, inc=1, device_id=(t - k, lax.rem(p + d, pn)), device_id_type=MESH
+                )
+
     def pair_copy(q, r):
         return pltpu.make_async_remote_copy(
             src_ref=part.at[q * slab + r], dst_ref=pair_buf.at[q // 2, r],
@@ -274,6 +285,20 @@
             src_ref=g_col.at[source], dst_ref=g_col.at[source],
             send_sem=g_send.at[target], recv_sem=g_recv.at[source],
             device_id=(target, p), device_id_type=MESH,
+        )
+
+    def g_next(k, d):
+        return pltpu.make_async_remote_copy(
+            src_ref=g_col.at[t], dst_ref=g_near.at[k - 1, p],
+            send_sem=near_send.at[k - 1], recv_sem=near_recv.at[k - 1],
+            device_id=(t + k, lax.rem(p + d, pn)), device_id_type=MESH,
+        )
+
+    def g_nears(k):
+        return pltpu.make_async_remote_copy(
+            src_ref=g_near.at[k - 1], dst_ref=g_near.at[k - 1],
+            send_sem=near_send.at[k - 1], recv_sem=near_recv.at[k - 1],
+            device_id=(t, partner), device_id_type=MESH,
         )
 
     def g_share(d):
@@ -344,7 +369,7 @@
     for x in range(length):
         psi_ref[x] = psi_ref[x] * occ
     table_load.wait()
-    pl.semaphore_wait(barrier, tn + pn - 2)
+    pl.semaphore_wait(barrier, tn + pn - 2 + (pn - 1) * jnp.minimum(NEAR, tn - 1 - t))
     t_sends(start)
 
     @pl.loop(0, length // MIDDLE)
@@ -417,6 +442,11 @@
         @pl.when(s > t)
         def clear():
             a_buf[s] = jnp.zeros(a_buf.shape[1:], jnp.float32)
+
+    for s in range(tn):
+
+        @pl.when((s > t) | ((s < t) & (s >= t - NEAR)))
+        def unused():
             g_col[s] = jnp.zeros(g_col.shape[1:], jnp.float32)
 
     gram_ref[...] = jnp.zeros_like(gram_ref)
@@ -453,9 +483,16 @@
     fold = 128 // total_rows
     short = rows // fold
     g_col[t] = jnp.concatenate([gram[i * short : (i + 1) * short] for i in range(fold)], axis=1)
+    for k in reversed(range(1, NEAR + 1)):
+
+        @pl.when(t + k < tn)
+        def upper():
+            for d in reversed(range(pn)):
+                g_next(k, d).start()
+
     for target in reversed(range(1, tn)):
 
-        @pl.when(t < target)
+        @pl.when(t + NEAR < target)
         def upward():
             g_up(t, target).start()
 
@@ -477,7 +514,7 @@
 
     for s in range(tn - 1):
 
-        @pl.when(t > s)
+        @pl.when(t > s + NEAR)
         def below():
             g_up(s, t).wait_recv()
 
@@ -486,20 +523,42 @@
     g_buf[p] = g_col[...]
     for target in range(1, tn):
 
-        @pl.when(t < target)
+        @pl.when(t + NEAR < target)
         def ended():
             g_up(t, target).wait_send()
+
+    for k in range(1, NEAR + 1):
+
+        @pl.when(t + k < tn)
+        def passed():
+            g_nears(k).wait_send()
 
     for r in range(slab - HELD):
         a_route(r, sent, False)
         a_onward(r, sent, False, False)
     g_shares().wait_recv()
+
+    for k in range(1, NEAR + 1):
+
+        @pl.when(t >= k)
+        def lower():
+            g_nears(k).wait_recv()
+
     blocks = []
     summed = g_buf[0]
     for q in range(1, pn):
         summed = summed + g_buf[q]
+    near = []
+    for k in range(NEAR):
+        total = g_near[k, 0]
+        for q in range(1, pn):
+            total = total + g_near[k, q]
+        near.append(total)
     for s in range(tn):
-        blocks += [summed[s, :, i * total_rows : (i + 1) * total_rows] for i in range(fold)]
+        piece = summed[s]
+        for k in range(NEAR):
+            piece = piece + jnp.where(t == s + k + 1, near[k], 0.0)
+        blocks += [piece[:, i * total_rows : (i + 1) * total_rows] for i in range(fold)]
     square = jnp.concatenate(blocks, axis=0)
     square = jnp.concatenate(
         [square, jnp.zeros((total_rows, width - total_rows), jnp.float32)], axis=1
@@ -613,6 +672,7 @@
             block,
             pltpu.VMEM((rows, total_rows), jnp.float32),
             pltpu.VMEM((tn, rows * total_rows // 128, 128), jnp.float32),
+            pltpu.VMEM((NEAR, pn, rows * total_rows // 128, 128), jnp.float32),
             pltpu.VMEM((pn, tn, rows * total_rows // 128, 128), jnp.float32),
             pltpu.VMEM((total_rows, width), jnp.float32),
         ],

time: 25.5 us -> 25.9 us (1.016)
  Pallas kernels: 23.3 us -> 23.7 us
    pallas_call x1, Pallas kernels: 23.3 us -> 23.7 us  [shards(): pl.pallas_call(functools.partial(kernel, tn, pn), out_shape=pltpu.VMEM((r...]
where the time goes in v7:
time: 25.9 us; the launch traced here: 25.7 us
  Pallas kernels  23.7 us (92%)
  between operations  1.3 us (5%)
  local copies, waits for them, and re-layouts  0.66 us (3%)
    pallas_call x1, Pallas kernels, shards(): pl.pallas_call(functools.partial(kernel, tn, pn), out_shape=pltpu.VMEM((r...  23.7 us
    unnamed x1, local copies, waits for them, and re-layouts  0.66 us

profile of v7, /device:TPU:25, one launch (start us, length us, event | category | flops | bytes accessed | tf_op | source)
XLA Modules:
  0.0 25.7 jit_solution(5366982453192980522)
XLA Ops:
  1.3 23.7 %exchange.1 = f32[8,4,1024]{2,1,0:T(4,128)S(1)} custom-call(f32[8,32,1024]{2,1,0:T(8,128)} %t_hbm.1, f32[32,32,128]{2,1,0:T(8,128)} %psi_hbm.1, bf16[256,256]{1,0:T(8,128)(2,1)} %constant.4.clone.weights_hbm, f32[32,17,128]{2,1,0:T(8,128)} %constant.5.clone.table_hbm, s32[1]{0:T(128)S(6)} %copy.9.occupied_ref, s32[1]{0:T(128)S(6)} %copy.10.retained_ref), custom_call_target="tpu_custom_call" | custom-call | tf_op jit(solution)/shard_map/exchange/pallas_call | solution.py:657
  25.0 0.7 %copy.8 = f32[8,4,1024]{2,1,0:T(4,128)} copy(f32[8,4,1024]{2,1,0:T(4,128)S(1)} %exchange.1) | data formatting | bytes 262144
